TPU v7x, 32 devices: a whole 2x2x4 slice. The times are simulated.
32 devices in a mesh: row: 8 (over y, x, core), col: 4 (over z).
Axes of the slice: x: 2, y: 2, z: 4, core: 2. Of those that a mesh axis runs over, the one named last changes fastest.
Arguments:
- diag_blocks: float32 [16, 512, 512], P('row', None, 'col'), as said below
- near_blocks: float32 [16, 4, 512, 512], P('row', None, None, 'col'), may hold values from -0.1 to 0.1, as said below
- cluster_bases: float32 [16, 512, 512], P('row', 'col'), as said below
- near_ids: int32 [16, 4], P('row'), may hold values from 0 to 15, as said below
- near_count: int32 [16], P('row'), may hold values from 1 to 4
- parent_bases: float32 [8, 512, 512], P('row'), as said below
Outputs:
- leaf_diag: float32 [16, 256, 256], P('row', None, 'col')
- leaf_near: float32 [16, 4, 256, 256], P('row', None, None, 'col')
- parent_diag: float32 [8, 256, 256], P('row', None, 'col')
Inputs may be any that keep to these rules, and one draw needn't show every extreme that they name: `near_ids`: slot 0 of cluster i names its sibling: i + 2 when i // 2 is even, else i - 2. The other slots may name any cluster. For sibling clusters a and b = a + 2 (a // 2 even), near_blocks[b, 0] is the transpose of near_blocks[a, 0]. `diag_blocks`: Symmetric. `cluster_bases`: the identity plus a small full-rank perturbation. `parent_bases`: the identity plus a small full-rank perturbation.
All inputs are finite; a program needn't handle non-finite values.
Results may differ from a plain program's by a relative error of at most 0.0003.
Values sent between devices are 32-bit elements; how exact they have to be, the bound alone decides.
No kernel may reach another device: no remote copies, remote signals or barrier semaphores. Data moves between devices by JAX's collectives and lax.ppermute only.
A program may use at most 128 MiB of HBM per device.

v0:
```python
import jax
import jax.numpy as jnp
from jax import lax
from jax.sharding import PartitionSpec as P

B = 512
K = 256
NEAR = 4
highest = lax.Precision.HIGHEST


def partner(shard, axis, apart):
    return lax.ppermute(shard, axis, [(i, i ^ 1 << apart) for i in range(lax.axis_size(axis))])


def eliminate(dense, redundant):
    factor = jnp.linalg.cholesky(dense[:redundant, :redundant])
    solved = jax.scipy.linalg.cho_solve((factor, True), dense[:redundant, redundant:])
    schur = dense[redundant:, redundant:] - jnp.dot(
        dense[redundant:, :redundant], solved, precision=highest
    )
    return (solved, schur)


def per_device(diag_blocks, near_blocks, cluster_bases, near_ids, near_count, parent_bases):
    clusters = diag_blocks.shape[0]
    redundant = B - K
    column = lax.axis_index("col")
    quarter = K // lax.axis_size("col")
    own_rows = cluster_bases.shape[1]
    full_bases = lax.all_gather(cluster_bases, "col", axis=1, tiled=True)
    partial_value = jnp.einsum("cij,cjk->cik", diag_blocks, cluster_bases, precision=highest)
    summed = lax.psum(partial_value, "col")
    dense = jnp.einsum("cji,cjk->cik", full_bases, summed, precision=highest)
    solved, schur = jax.vmap(lambda single: eliminate(single, redundant))(dense)
    leaf_diag = lax.dynamic_slice_in_dim(schur, column * quarter, quarter, 2)
    flat_ids = near_ids.reshape(-1)
    shards = lax.all_gather(cluster_bases[:, :, redundant:], "row", axis=0, tiled=True)
    number = shards.shape[0]
    one_hot = (flat_ids[:, None] == jnp.arange(number, dtype=jnp.int32)[None, :]).astype(
        jnp.float32
    )
    picked = jnp.dot(one_hot, shards.reshape(number, -1), precision=highest)
    picked = picked.reshape(clusters, NEAR, own_rows, K)
    terms = jnp.einsum("cnij,cnjk->cnik", near_blocks, picked, precision=highest)
    right_part = lax.psum_scatter(terms, "col", scatter_dimension=3, tiled=True)
    moved = jnp.einsum("cji,cnjk->cnik", full_bases, right_part, precision=highest)
    coupled = moved[:, :, redundant:, :] - jnp.einsum(
        "cri,cnrk->cnik", solved, moved[:, :, :redundant, :], precision=highest
    )
    live = (jnp.arange(NEAR, dtype=jnp.int32)[None, :] < near_count[:, None]).astype(jnp.float32)
    leaf_near = coupled * live[:, :, None, None]
    halfway = clusters // 2
    parity = lax.axis_index("row") % 2
    stacked = jnp.stack([leaf_diag, leaf_near[:, 0]])
    kept = lax.dynamic_slice_in_dim(stacked, parity * halfway, halfway, 1)
    outgoing = lax.dynamic_slice_in_dim(stacked, (1 - parity) * halfway, halfway, 1)
    arrived = partner(outgoing, "row", 0)
    first_child = jnp.where(parity == 0, kept, arrived)
    second_child = jnp.where(parity == 0, arrived, kept)
    left_columns = jnp.concatenate([first_child[0], second_child[1]], axis=1)
    right_columns = jnp.concatenate([first_child[1], second_child[0]], axis=1)
    merged = jnp.concatenate([left_columns, right_columns], axis=2)
    rows_first = lax.dynamic_slice_in_dim(parent_bases, column * quarter, quarter, 1)
    rows_second = lax.dynamic_slice_in_dim(parent_bases, K + column * quarter, quarter, 1)
    chosen_rows = jnp.concatenate([rows_first, rows_second], axis=1)
    lifted = jnp.einsum("hji,hjk->hik", parent_bases, merged, precision=highest)
    parent_part = jnp.einsum("hij,hjk->hik", lifted, chosen_rows, precision=highest)
    parent_dense = lax.psum(parent_part, "col")
    parent_schur = jax.vmap(lambda single: eliminate(single, K)[1])(parent_dense)
    parent_diag = lax.dynamic_slice_in_dim(parent_schur, column * quarter, quarter, 2)
    return (leaf_diag, leaf_near, parent_diag)


def solution(mesh):
    return jax.shard_map(
        per_device,
        mesh=mesh,
        in_specs=(
            P("row", None, "col"),
            P("row", None, None, "col"),
            P("row", "col", None),
            P("row", None),
            P("row"),
            P("row", None, None),
        ),
        out_specs=(P("row", None, "col"), P("row", None, None, "col"), P("row", None, "col")),
        check_vma=False,
    )
```

profile of v0, /device:TPU:0, one launch (start us, length us, event | category | flops | bytes accessed | tf_op | source)
XLA Modules:
  0.0 401.4 jit_solution(10855884119777863552)
XLA Ops:
  8.1 1.8 slice.175
  9.9 4.4 %fusion.60 = f32[2,512,512]{2,1,0:T(8,128)} fusion(f32[2,512,128]{2,1,0:T(8,128)} %param.6, f32[2,128,512]{2,1,0:T(8,128)} %param.8), kind=kOutput, calls=%fused_computation.129 | convolution fusion | flops 805306368 | bytes 3145728 | tf_op jit(solution)/shard_map/cij,cjk->cik/dot_general | solution.py:32
  15.1 26.7 %all-gather.5.cloned.1.call-done = f32[16,128,256]{2,1,0:T(8,128)} async-done(((f32[2,128,256]{2,1,0:T(8,128)}), f32[16,128,256]{2,1,0:T(8,128)}) %all-gather.5.cloned.1.call-update) | async-done | bytes 2097168 | tf_op jit(solution)/shard_map/all_gather | solution.py:38
  41.8 3.8 fusion
  45.7 5.1 %convolution_bitcast_fusion = f32[2,4,512,256]{2,3,1,0:T(8,128)} fusion(f32[2,4,512,128]{3,2,1,0:T(8,128)S(1)} %copy-done, f32[2,4,128,256]{3,1,2,0:T(4,128)S(1)} %fusion), kind=kOutput, calls=%fused_computation.4 | convolution fusion | flops 1610612736 | bytes 7340032 | tf_op jit(solution)/shard_map/cnij,cnjk->cnik/dot_general | solution.py:45
  51.5 75.6 %all-reduce.5.cloned.1.call-done = f32[2,512,512]{2,1,0:T(8,128)} async-done(((f32[2,512,512]{2,1,0:T(8,128)}), f32[2,512,512]{2,1,0:T(8,128)}) %all-reduce.5.cloned.1.call-update) | async-done | bytes 2097168 | tf_op jit(solution)/shard_map/psum | solution.py:33
  127.1 5.7 %convolution_bitcast_fusion.1 = f32[2,512,512]{1,2,0:T(8,128)S(1)} fusion(f32[2,512,512]{2,1,0:T(8,128)} %all-reduce.5.cloned.1.call-done, f32[2,512,512]{2,1,0:T(8,128)} %all-gather.3.cloned.1.call-done), kind=kOutput, calls=%fused_computation.10 | convolution fusion | flops 3221225472 | bytes 6291456 | tf_op jit(solution)/shard_map/cji,cjk->cik/dot_general | solution.py:34
  137.3 23.9 %custom-call.40 = f32[2,128,128]{2,1,0:T(8,128)S(1)} custom-call(f32[2,128,128]{2,1,0:T(8,128)S(1)} %cholesky.239), custom_call_target="Cholesky" | custom-call | tf_op jit(solution)/shard_map/vmap(jit(cholesky))/cholesky | solution.py:17
  161.3 19.7 %custom-call.41 = f32[2,1,128,128]{2,3,1,0:T(8,128)S(1)} custom-call(f32[2,1,128,128]{3,2,1,0:T(8,128)S(1)} %select_bitcast_fusion), custom_call_target="InvertDiagBlocksLowerTriangular" | custom-call | tf_op jit(solution)/shard_map/vmap(jit(cholesky))/cholesky | solution.py:17
  183.4 23.5 %custom-call.42 = f32[2,128,128]{2,1,0:T(8,128)S(1)} custom-call(f32[2,128,128]{2,1,0:T(8,128)S(1)} %convolution_subtract_fusion.3), custom_call_target="Cholesky" | custom-call | tf_op jit(solution)/shard_map/vmap(jit(cholesky))/cholesky | solution.py:17
  207.3 3.9 while.2
  211.2 39.5 %custom-call.43 = f32[2,2,128,128]{2,3,1,0:T(8,128)S(1)} custom-call(f32[2,2,128,128]{3,2,1,0:T(8,128)S(1)} %bitcast.192), custom_call_target="InvertDiagBlocksLowerTriangular" | custom-call | tf_op jit(solution)/shard_map/vmap(jit(_cho_solve))/triangular_solve | solution.py:18
  255.3 2.1 fusion.16
  258.4 3.9 fusion.4
  267.0 2.0 convolution_bitcast_fusion.2
  269.1 51.3 %all-reduce.7.cloned.1.call-done = f32[1,512,512]{1,2,0:T(8,128)} async-done(((f32[1,512,512]{1,2,0:T(8,128)}), f32[1,512,512]{1,2,0:T(8,128)}) %all-reduce.7.cloned.1.call-update) | async-done | bytes 1048592 | tf_op jit(solution)/shard_map/psum | solution.py:69
  320.4 1.9 fusion.59
  325.2 11.7 %custom-call.44 = f32[1,128,128]{2,1,0:T(8,128)S(1)} custom-call(f32[1,128,128]{2,1,0:T(8,128)S(1)} %cholesky.242), custom_call_target="Cholesky" | custom-call | tf_op jit(solution)/shard_map/vmap(jit(cholesky))/cholesky | solution.py:17
  337.0 10.0 %custom-call.45 = f32[1,1,128,128]{2,3,1,0:T(8,128)S(1)} custom-call(f32[1,1,128,128]{3,2,1,0:T(8,128)S(1)} %get-tuple-element.57), custom_call_target="InvertDiagBlocksLowerTriangular" | custom-call | tf_op jit(solution)/shard_map/vmap(jit(cholesky))/cholesky | solution.py:17
  349.1 11.7 %custom-call.46 = f32[1,128,128]{2,1,0:T(8,128)S(1)} custom-call(f32[1,128,128]{2,1,0:T(8,128)S(1)} %fusion.11), custom_call_target="Cholesky" | custom-call | tf_op jit(solution)/shard_map/vmap(jit(cholesky))/cholesky | solution.py:17
  364.3 5.3 %while.3 = (s32[]{:T(128)}, f32[1,256,256]{2,1,0:T(8,128)S(1)}, s32[2,2]{1,0:T(2,128)S(1)}, f32[2,1,128,128]{3,2,1,0:T(8,128)}, s32[]{:T(128)}) while((s32[]{:T(128)}, f32[1,256,256]{2,1,0:T(8,128)S(1)}, s32[2,2]{1,0:T(2,128)S(1)}, f32[2,1,128,128]{3,2,1,0:T(8,128)}, s32[]{:T(128)}) %tuple.66), condition=%wide.while_cond.1, body=%wide.while_body.1.sunk | while | flops 2 | bytes 132205 | solution.py:18
  365.0 2.0 bitcast_dynamic-update-slice_fusion.6
  367.6 2.0 bitcast_dynamic-update-slice_fusion.6
  369.6 20.5 %custom-call.47 = f32[1,2,128,128]{2,3,1,0:T(8,128)S(1)} custom-call(f32[1,2,128,128]{3,2,1,0:T(8,128)} %bitcast.193), custom_call_target="InvertDiagBlocksLowerTriangular" | custom-call | tf_op jit(solution)/shard_map/vmap(jit(_cho_solve))/triangular_solve | solution.py:18
  (100 shorter events, 35.6 us)
Async XLA Ops:
  8.0 37.7 %copy-start = (f32[2,4,512,128]{3,2,1,0:T(8,128)S(1)}, f32[2,4,512,128]{3,2,1,0:T(8,128)}, u32[]{:S(2)}) copy-start(f32[2,4,512,128]{3,2,1,0:T(8,128)} %param.7) | copy-start | bytes 6291460
  8.0 33.8 %all-gather.5.cloned.1.call-start = ((), (), s32[]{:S(2)}) async-start(), calls=%async_computation.3 | async-start | bytes 2359296 | tf_op jit(solution)/shard_map/all_gather | solution.py:38
  9.9 117.2 %all-reduce.5.cloned.1.call-start = ((), (), s32[]{:S(2)}) async-start(), calls=%async_computation.1 | async-start | bytes 4194304 | tf_op jit(solution)/shard_map/psum | solution.py:33
  14.3 27.5 %copy-start.9 = (s32[2,4]{1,0:T(2,128)S(1)}, s32[2,4]{1,0:T(2,128)}, u32[]{:S(2)}) copy-start(s32[2,4]{1,0:T(2,128)} %param.9) | copy-start | bytes 100
  14.3 112.8 %all-gather.3.cloned.1.call-start = ((), (), s32[]{:S(2)}) async-start(), calls=%async_computation.2 | async-start | bytes 2621440 | tf_op jit(solution)/shard_map/all_gather | solution.py:31
  15.1 243.3 %reduce-scatter.2.cloned.1.call-start = ((), (), s32[]{:S(2)}) async-start(), calls=%async_computation.4 | async-start | bytes 5242880 | tf_op jit(solution)/shard_map/reduce_scatter | solution.py:46
  50.8 0.7 copy-start.10
  50.8 269.6 %all-reduce.7.cloned.1.call-start = ((), (), s32[]{:S(2)}) async-start(), calls=%async_computation.5 | async-start | bytes 2097152 | tf_op jit(solution)/shard_map/psum | solution.py:69
  132.8 1.3 copy-start.1
  136.4 0.8 copy-start.4
  258.3 7.0 %copy-start.5 = (f32[2,256,64]{1,2,0:T(8,128)}, f32[2,256,64]{1,2,0:T(8,128)S(1)}, u32[]{:S(2)}) copy-start(f32[2,256,64]{1,2,0:T(8,128)S(1)} %dynamic-slice_subtract_fusion) | copy-start | bytes 393220
  262.9 0.8 copy-start.7
  263.7 2.6 copy-start.3
  263.8 1.5 collective-permute-start
  322.3 67.8 %copy-start.2 = (f32[1,512,512]{1,2,0:T(8,128)S(1)}, f32[1,512,512]{1,2,0:T(8,128)}, u32[]{:S(2)}) copy-start(f32[1,512,512]{1,2,0:T(8,128)} %all-reduce.7.cloned.1.call-done) | copy-start | bytes 3145732
  324.5 0.7 copy-start.8
  361.5 1.9 copy-start.6
Sparse Core Ops, SparseCore 0:
  11.3 30.4 all-gather.4
  43.4 72.8 all-gather.2
  269.2 51.1 all-reduce.6
Sparse Core Ops, SparseCore 1:
  14.4 112.6 all-reduce.4
  129.3 75.8 reduce-scatter.1
where the time goes:
time: 410 us; the launch traced here: 401 us
  other arithmetic  169 us (41%)
  waiting for transfers between devices  155 us (38%)
  matrix products  40 us (10%)
  local copies, waits for them, and re-layouts  20.5 us (5%)
  between operations  17.1 us (4%)
    another operation x16, other arithmetic, eliminate(): factor = jnp.linalg.cholesky(dense[:redundant, :redundant])  102 us
    psum x1, waiting for transfers between devices, per_device(): summed = lax.psum(partial_value, 'col')  75.6 us
    another operation x6, other arithmetic, eliminate(): jax.scipy.linalg.cho_solve((factor, True), dense[:redundant, redundant:])  61.1 us
    psum x1, waiting for transfers between devices, per_device(): parent_dense = lax.psum(parent_part, 'col')  51.3 us
    all_gather x1, waiting for transfers between devices, per_device(): lax.all_gather(cluster_bases[:, :, redundant:], 'row', axis=0, tiled=True)  26.7 us
    another operation x12, local copies, waits for them, and re-layouts  9.11 us
  transfers between devices with their start and end apart: 6, of which 4 were waited for; matrix products, arithmetic and copies ran while one was open for 36% of the time, Pallas kernels for 0%

commit v1 on v0

--- a/solution.py
+++ b/solution.py
@@ -30,7 +30,9 @@
     own_rows = cluster_bases.shape[1]
     full_bases = lax.all_gather(cluster_bases, "col", axis=1, tiled=True)
     partial_value = jnp.einsum("cij,cjk->cik", diag_blocks, cluster_bases, precision=highest)
-    summed = lax.psum(partial_value, "col")
+    summed = partial_value
+    for hop in (1, 2):
+        summed = summed + lax.ppermute(summed, "col", [(dev, dev ^ hop) for dev in range(4)])
     dense = jnp.einsum("cji,cjk->cik", full_bases, summed, precision=highest)
     solved, schur = jax.vmap(lambda single: eliminate(single, redundant))(dense)
     leaf_diag = lax.dynamic_slice_in_dim(schur, column * quarter, quarter, 2)

time: 410 us -> 536 us (1.31)
  waiting for transfers between devices: 155 us -> 272 us
  starting transfers between devices: 0.28 us -> 8.71 us
    ppermute x0 -> x2, waiting for transfers between devices: none -> 194 us  [per_device(): lax.ppermute(summed, 'col', [(dev, dev ^ hop) for dev in range(4)])]
    psum x1 -> x0, waiting for transfers between devices: 75.6 us -> none  [per_device(): summed = lax.psum(partial_value, 'col')]
    ppermute x0 -> x2, starting transfers between devices: none -> 8.18 us  [per_device(): lax.ppermute(summed, 'col', [(dev, dev ^ hop) for dev in range(4)])]
  transfers between devices with their start and end apart: 6 -> 7, of which waited for: 4 -> 6; matrix products, arithmetic and copies ran while one was open for 36% -> 28% of each run, Pallas kernels for 0% -> 0%
where the time goes in v1:
time: 536 us; the launch traced here: 531 us
  waiting for transfers between devices  272 us (51%)
  other arithmetic  174 us (32%)
  matrix products  39.6 us (7%)
  local copies, waits for them, and re-layouts  20.4 us (4%)
  between operations  15.7 us (3%)
  starting transfers between devices  8.71 us (2%)
    ppermute x2, waiting for transfers between devices, per_device(): lax.ppermute(summed, 'col', [(dev, dev ^ hop) for dev in range(4)])  194 us
    another operation x16, other arithmetic, eliminate(): factor = jnp.linalg.cholesky(dense[:redundant, :redundant])  103 us
    another operation x6, other arithmetic, eliminate(): jax.scipy.linalg.cho_solve((factor, True), dense[:redundant, redundant:])  61.9 us
    psum x1, waiting for transfers between devices, per_device(): parent_dense = lax.psum(parent_part, 'col')  53 us
    all_gather x1, waiting for transfers between devices, per_device(): lax.all_gather(cluster_bases[:, :, redundant:], 'row', axis=0, tiled=True)  23.7 us
  transfers between devices with their start and end apart: 7, of which 6 were waited for; matrix products, arithmetic and copies ran while one was open for 28% of the time, Pallas kernels for 0%

profile of v1, /device:TPU:0, one launch (start us, length us, event | category | flops | bytes accessed | tf_op | source)
XLA Modules:
  0.0 530.8 jit_solution(7468563825464074832)
XLA Ops:
  9.9 4.4 fusion.66
  14.2 3.1 collective-permute-start
  17.3 23.7 %all-gather.5.cloned.1.call-done = f32[16,128,256]{2,1,0:T(8,128)} async-done(((f32[2,128,256]{2,1,0:T(8,128)}), f32[16,128,256]{2,1,0:T(8,128)}) %all-gather.5.cloned.1.call-update) | async-done | bytes 2097168 | tf_op jit(solution)/shard_map/all_gather | solution.py:40
  41.0 3.8 fusion
  44.8 5.1 convolution_bitcast_fusion
  50.3 39.1 %collective-permute-done = f32[2,512,512]{2,1,0:T(8,128)} collective-permute-done((f32[2,512,512]{2,1,0:T(8,128)}, f32[2,512,512]{2,1,0:T(8,128)}, u32[]{:S(2)}, u32[]{:S(2)}) %collective-permute-start) | collective-permute-done | bytes 2097184 | tf_op jit(solution)/shard_map/ppermute | solution.py:35
  89.4 4.1 add.86
  93.5 5.1 collective-permute-start.1
  99.5 154.4 %collective-permute-done.1 = f32[2,512,512]{2,1,0:T(8,128)} collective-permute-done((f32[2,512,512]{2,1,0:T(8,128)}, f32[2,512,512]{2,1,0:T(8,128)}, u32[]{:S(2)}, u32[]{:S(2)}) %collective-permute-start.1) | collective-permute-done | bytes 2097184 | tf_op jit(solution)/shard_map/ppermute | solution.py:35
  253.9 6.2 %fusion.6 = f32[2,512,512]{1,2,0:T(8,128)S(1)} fusion(f32[2,512,512]{2,1,0:T(8,128)} %all-gather.3.cloned.1.call-done, f32[2,512,512]{2,1,0:T(8,128)} %add.86, f32[2,512,512]{2,1,0:T(8,128)} %collective-permute-done.1), kind=kOutput, calls=%fused_computation.12 | convolution fusion | flops 3221749760 | bytes 8388608 | tf_op jit(solution)/shard_map/cji,cjk->cik/dot_general | solution.py:36
  263.7 23.5 %custom-call.40 = f32[2,128,128]{2,1,0:T(8,128)S(1)} custom-call(f32[2,128,128]{2,1,0:T(8,128)S(1)} %cholesky.239), custom_call_target="Cholesky" | custom-call | tf_op jit(solution)/shard_map/vmap(jit(cholesky))/cholesky | solution.py:17
  287.2 20.3 %custom-call.41 = f32[2,1,128,128]{2,3,1,0:T(8,128)} custom-call(f32[2,1,128,128]{3,2,1,0:T(8,128)S(1)} %select_bitcast_fusion), custom_call_target="InvertDiagBlocksLowerTriangular" | custom-call | tf_op jit(solution)/shard_map/vmap(jit(cholesky))/cholesky | solution.py:17
  309.1 24.0 %custom-call.42 = f32[2,128,128]{2,1,0:T(8,128)S(1)} custom-call(f32[2,128,128]{2,1,0:T(8,128)S(1)} %convolution_subtract_fusion.2), custom_call_target="Cholesky" | custom-call | tf_op jit(solution)/shard_map/vmap(jit(cholesky))/cholesky | solution.py:17
  333.5 5.1 while.2
  338.7 40.3 %custom-call.43 = f32[2,2,128,128]{2,3,1,0:T(8,128)S(1)} custom-call(f32[2,2,128,128]{3,2,1,0:T(8,128)} %bitcast.190), custom_call_target="InvertDiagBlocksLowerTriangular" | custom-call | tf_op jit(solution)/shard_map/vmap(jit(_cho_solve))/triangular_solve | solution.py:18
  383.5 2.1 fusion.21
  386.6 3.9 fusion.9
  395.2 2.0 convolution_bitcast_fusion.1
  397.3 53.0 %all-reduce.4.cloned.1.call-done = f32[1,512,512]{1,2,0:T(8,128)} async-done(((f32[1,512,512]{1,2,0:T(8,128)}), f32[1,512,512]{1,2,0:T(8,128)}) %all-reduce.4.cloned.1.call-update) | async-done | bytes 1048592 | tf_op jit(solution)/shard_map/psum | solution.py:71
  455.1 11.7 %custom-call.44 = f32[1,128,128]{2,1,0:T(8,128)S(1)} custom-call(f32[1,128,128]{2,1,0:T(8,128)S(1)} %cholesky.242), custom_call_target="Cholesky" | custom-call | tf_op jit(solution)/shard_map/vmap(jit(cholesky))/cholesky | solution.py:17
  466.8 10.0 %custom-call.45 = f32[1,1,128,128]{2,3,1,0:T(8,128)S(1)} custom-call(f32[1,1,128,128]{3,2,1,0:T(8,128)S(1)} %get-tuple-element.57), custom_call_target="InvertDiagBlocksLowerTriangular" | custom-call | tf_op jit(solution)/shard_map/vmap(jit(cholesky))/cholesky | solution.py:17
  479.0 11.7 %custom-call.46 = f32[1,128,128]{2,1,0:T(8,128)S(1)} custom-call(f32[1,128,128]{2,1,0:T(8,128)S(1)} %fusion.16), custom_call_target="Cholesky" | custom-call | tf_op jit(solution)/shard_map/vmap(jit(cholesky))/cholesky | solution.py:17
  494.3 5.3 while.3
  499.6 20.5 %custom-call.47 = f32[1,2,128,128]{2,3,1,0:T(8,128)S(1)} custom-call(f32[1,2,128,128]{3,2,1,0:T(8,128)} %bitcast.191), custom_call_target="InvertDiagBlocksLowerTriangular" | custom-call | tf_op jit(solution)/shard_map/vmap(jit(_cho_solve))/triangular_solve | solution.py:18
  (100 shorter events, 43.2 us)
Async XLA Ops:
  7.2 37.7 %copy-start = (f32[2,4,512,128]{3,2,1,0:T(8,128)S(1)}, f32[2,4,512,128]{3,2,1,0:T(8,128)}, u32[]{:S(2)}) copy-start(f32[2,4,512,128]{3,2,1,0:T(8,128)} %param.7) | copy-start | bytes 6291460
  7.2 33.8 %all-gather.5.cloned.1.call-start = ((), (), s32[]{:S(2)}) async-start(), calls=%async_computation.2 | async-start | bytes 2359296 | tf_op jit(solution)/shard_map/all_gather | solution.py:40
  9.0 31.9 %copy-start.8 = (s32[2,4]{1,0:T(2,128)S(1)}, s32[2,4]{1,0:T(2,128)}, u32[]{:S(2)}) copy-start(s32[2,4]{1,0:T(2,128)} %param.9) | copy-start | bytes 100
  9.1 90.4 %all-gather.3.cloned.1.call-start = ((), (), s32[]{:S(2)}) async-start(), calls=%async_computation.1 | async-start | bytes 2621440 | tf_op jit(solution)/shard_map/all_gather | solution.py:31
  9.8 376.8 %reduce-scatter.2.cloned.1.call-start = ((), (), s32[]{:S(2)}) async-start(), calls=%async_computation.3 | async-start | bytes 5242880 | tf_op jit(solution)/shard_map/reduce_scatter | solution.py:48
  14.2 75.2 %collective-permute-start = (f32[2,512,512]{2,1,0:T(8,128)}, f32[2,512,512]{2,1,0:T(8,128)}, u32[]{:S(2)}, u32[]{:S(2)}) collective-permute-start(f32[2,512,512]{2,1,0:T(8,128)} %fusion.66), channel_id=1, source_target_pairs={{0,1},{1,0},{2,3},{3,2},{4,5},{5,4},{6,7},{7,6},{8,9},{9,8},{10,11... | collective-permute-start | bytes 6291464 | tf_op jit(solution)/shard_map/ppermute | solution.py:35
  50.0 48.8 %copy-start.9 = (s32[2]{0:T(128)S(1)}, s32[2]{0:T(128)}, u32[]{:S(2)}) copy-start(s32[2]{0:T(128)} %param.10) | copy-start | bytes 28
  50.0 400.3 %all-reduce.4.cloned.1.call-start = ((), (), s32[]{:S(2)}) async-start(), calls=%async_computation.4 | async-start | bytes 2097152 | tf_op jit(solution)/shard_map/psum | solution.py:71
  93.5 160.4 %collective-permute-start.1 = (f32[2,512,512]{2,1,0:T(8,128)}, f32[2,512,512]{2,1,0:T(8,128)}, u32[]{:S(2)}, u32[]{:S(2)}) collective-permute-start(f32[2,512,512]{2,1,0:T(8,128)} %add.86), channel_id=1, source_target_pairs={{0,2},{1,3},{2,0},{3,1},{4,6},{5,7},{6,4},{7,5},{8,10},{9,11},{10,... | collective-permute-start | bytes 6291464 | tf_op jit(solution)/shard_map/ppermute | solution.py:35
  260.1 1.3 copy-start.1
  386.6 7.0 %copy-start.4 = (f32[2,256,64]{1,2,0:T(8,128)}, f32[2,256,64]{1,2,0:T(8,128)S(1)}, u32[]{:S(2)}) copy-start(f32[2,256,64]{1,2,0:T(8,128)S(1)} %dynamic-slice_subtract_fusion) | copy-start | bytes 393220
  391.2 0.8 copy-start.6
  392.0 2.6 copy-start.3
  392.0 1.5 collective-permute-start.2
  452.2 67.9 %copy-start.2 = (f32[1,512,512]{1,2,0:T(8,128)S(1)}, f32[1,512,512]{1,2,0:T(8,128)}, u32[]{:S(2)}) copy-start(f32[1,512,512]{1,2,0:T(8,128)} %all-reduce.4.cloned.1.call-done) | copy-start | bytes 3145732
  454.4 0.7 copy-start.7
  491.4 1.9 copy-start.5
Sparse Core Ops, SparseCore 0:
  10.4 30.4 all-gather.4
  42.6 56.8 all-gather.2
  101.8 130.0 reduce-scatter.1
  397.4 52.8 all-reduce.3
